TPU v7x, 128 devices: a whole 4x4x4 slice. The times are simulated.
128 devices in a mesh: req: 4 (over y), tp: 32 (over x, z, core).
Axes of the slice: x: 4, y: 4, z: 4, core: 2. Of those that a mesh axis runs over, the one named last changes fastest.
Arguments:
- hidden_states: bfloat16 [16, 4, 1024], P('req'), may hold values from -48 to 48
- lengths: int32 [16], P('req'), may hold values from 16 to 4096, as said below
- qkv_weight: bfloat16 [2048, 1024], P('tp'), may hold values from -1 to 1
- rotated_key_cache: bfloat16 [16, 4096, 512], P('req', 'tp'), may hold values from -1000 to 1000
- earlier_value_cache: bfloat16 [16, 4096, 512], P('req', 'tp'), may hold values from -16 to 16
- out_weight: bfloat16 [1024, 1024], P('tp'), may hold values from -0.1875 to 0.1875
- expert_ids: int32 [16, 4, 8], P('req'), may hold values from 0 to 31, all different within a row
- combine_weights: int32 [16, 4, 8], P('req'), may hold values from 4096 to 65535
- gate_up_weight: bfloat16 [32, 1024, 1024], P('tp'), may hold values from -0.1875 to 0.1875
- down_weight: bfloat16 [32, 512, 1024], P('tp'), may hold values from -0.25 to 0.25
Outputs:
- layer_output: bfloat16 [16, 4, 1024], P('req')
Inputs may be any that keep to these rules, and one draw needn't show every extreme that they name: `lengths`: cache length of each request; some request has exactly 4096. `expert_ids`: each token's 8 experts are distinct.
All inputs are finite; a program needn't handle non-finite values.
Results may differ from a plain program's by a relative error of at most 0.008.
Values may be sent and summed in bfloat16 or wider, within the bound.
A program may use at most 64 MiB of HBM per device.

v0:
```python
import jax
import jax.numpy as jnp
from jax import lax
from jax.sharding import PartitionSpec as P

QUERY_HEADS = 16
KEY_VALUE_HEADS = 8
HEAD_DIMENSION = 64
EPSILON = 1e-05
ROPE_BASE = 10000.0
NEGATIVE = -1e30


def merged(part, axis, combine):
    gathered = jax.tree.map(lambda a: lax.all_gather(a, axis), part)

    def take(source):
        return jax.tree.map(lambda a: lax.dynamic_index_in_dim(a, source, 0, False), gathered)

    return lax.fori_loop(
        1, lax.axis_size(axis), lambda source, state: combine(state, take(source)), take(0)
    )


def rms_rows(value_rows):
    return value_rows * lax.rsqrt(
        jnp.mean(value_rows * value_rows, axis=-1, keepdims=True) + EPSILON
    )


def apply_rotation(value_rows, position_index):
    half_width = value_rows.shape[-1] // 2
    rates = ROPE_BASE ** (-2.0 * jnp.arange(half_width, dtype=jnp.float32) / value_rows.shape[-1])
    angles = position_index[:, None, None] * rates
    cosine = jnp.cos(angles)
    sines = jnp.sin(angles)
    front_half = value_rows[..., :half_width]
    back_half = value_rows[..., half_width:]
    return jnp.concatenate(
        [front_half * cosine - back_half * sines, back_half * cosine + front_half * sines], axis=-1
    )


def join_parts(earlier, later):
    highest = jnp.maximum(earlier[0], later[0])
    scale_earlier = jnp.exp(earlier[0] - highest)
    scale_later = jnp.exp(later[0] - highest)
    weight_sum = earlier[1] * scale_earlier + later[1] * scale_later
    value_sum = earlier[2] * scale_earlier[..., None] + later[2] * scale_later[..., None]
    return (highest, weight_sum, value_sum)


def to_columns(value_rows, step_number, group_count):
    request_list, kv_heads, _, head_size = value_rows.shape
    return (
        value_rows.reshape(request_list, kv_heads, step_number, group_count, head_size)
        .transpose(0, 2, 1, 3, 4)
        .reshape(request_list * step_number, kv_heads * group_count * head_size)
    )


def expert_terms(normed, chosen, shares, gate_up_weight, down_weight, first_expert):
    ff_width = down_weight.shape[1]
    united_out = jnp.einsum(
        "nd,edf->enf", normed, gate_up_weight, preferred_element_type=jnp.float32
    )
    activation = (jax.nn.silu(united_out[..., :ff_width]) * united_out[..., ff_width:]).astype(
        jnp.bfloat16
    )
    outcome = jnp.einsum(
        "enf,efd->end", activation, down_weight, preferred_element_type=jnp.float32
    )
    owners = first_expert + jnp.arange(gate_up_weight.shape[0], dtype=jnp.int32)
    factors = jnp.sum(
        jnp.where(chosen[None, :, :] == owners[:, None, None], shares[None, :, :], 0.0), axis=-1
    )
    return jnp.sum(factors[:, :, None] * outcome, axis=0)


def per_device(
    hidden_states,
    lengths,
    qkv_weight,
    rotated_key_cache,
    earlier_value_cache,
    out_weight,
    expert_ids,
    combine_weights,
    gate_up_weight,
    down_weight,
):
    request_list, step_number, model_width = hidden_states.shape
    token_rows = request_list * step_number
    group_count = QUERY_HEADS // KEY_VALUE_HEADS
    query_total_width = QUERY_HEADS * HEAD_DIMENSION
    key_value_width = KEY_VALUE_HEADS * HEAD_DIMENSION
    score_scale = HEAD_DIMENSION ** (-0.5)
    inputs_flat = hidden_states.reshape(token_rows, model_width)
    normed = rms_rows(inputs_flat.astype(jnp.float32)).astype(jnp.bfloat16)
    projected_part = lax.dot_general(
        qkv_weight, normed, (((1,), (1,)), ((), ())), preferred_element_type=jnp.float32
    ).astype(jnp.bfloat16)
    projected_all = lax.all_gather(projected_part, "tp", axis=0, tiled=True)
    query_key_value_rows = projected_all.T
    position_index = (
        (lengths[:, None] + jnp.arange(step_number, dtype=jnp.int32)[None, :])
        .reshape(token_rows)
        .astype(jnp.float32)
    )
    query_rows = apply_rotation(
        query_key_value_rows[:, :query_total_width]
        .reshape(token_rows, QUERY_HEADS, HEAD_DIMENSION)
        .astype(jnp.float32),
        position_index,
    ).astype(jnp.bfloat16)
    fresh_keys = apply_rotation(
        query_key_value_rows[:, query_total_width : query_total_width + key_value_width]
        .reshape(token_rows, KEY_VALUE_HEADS, HEAD_DIMENSION)
        .astype(jnp.float32),
        position_index,
    ).astype(jnp.bfloat16)
    fresh_values = query_key_value_rows[:, query_total_width + key_value_width :].reshape(
        request_list, step_number, KEY_VALUE_HEADS, HEAD_DIMENSION
    )
    grouped_rows = (
        query_rows.reshape(request_list, step_number, KEY_VALUE_HEADS, group_count, HEAD_DIMENSION)
        .transpose(0, 2, 1, 3, 4)
        .reshape(request_list, KEY_VALUE_HEADS, step_number * group_count, HEAD_DIMENSION)
    )
    cache_extent = rotated_key_cache.shape[1]
    stored_keys = rotated_key_cache.reshape(
        request_list, cache_extent, KEY_VALUE_HEADS, HEAD_DIMENSION
    )
    stored_values = earlier_value_cache.reshape(
        request_list, cache_extent, KEY_VALUE_HEADS, HEAD_DIMENSION
    )
    scores = (
        jnp.einsum("bgqd,bcgd->bgqc", grouped_rows, stored_keys, preferred_element_type=jnp.float32)
        * score_scale
    )
    start_pos = lax.axis_index("tp") * cache_extent
    live_rows = (start_pos + jnp.arange(cache_extent, dtype=jnp.int32))[None, :] < lengths[:, None]
    live_mask = live_rows[:, None, None, :]
    masked = jnp.where(live_mask, scores, NEGATIVE)
    highest = jnp.max(masked, axis=-1)
    weights = jnp.where(live_mask, jnp.exp(masked - highest[..., None]), 0.0)
    weight_sum = jnp.sum(weights, axis=-1)
    value_sum = jnp.einsum(
        "bgqc,bcgd->bgqd",
        weights.astype(jnp.bfloat16),
        stored_values,
        preferred_element_type=jnp.float32,
    )
    feature_rows = out_weight.shape[0]
    column_begin = lax.axis_index("tp") * feature_rows
    top_score, total_all, sum_all = merged((highest, weight_sum, value_sum), "tp", join_parts)
    grouped_keys = fresh_keys.reshape(request_list, step_number, KEY_VALUE_HEADS, HEAD_DIMENSION)
    new_scores = (
        jnp.einsum(
            "bgqd,bsgd->bgqs", grouped_rows, grouped_keys, preferred_element_type=jnp.float32
        )
        * score_scale
    )
    query_step = jnp.arange(step_number * group_count, dtype=jnp.int32) // group_count
    causal = jnp.arange(step_number, dtype=jnp.int32)[None, :] <= query_step[:, None]
    new_masked = jnp.where(causal, new_scores, NEGATIVE)
    final_peak = jnp.maximum(top_score, jnp.max(new_masked, axis=-1))
    new_weights = jnp.where(causal, jnp.exp(new_masked - final_peak[..., None]), 0.0)
    carried = jnp.exp(top_score - final_peak)
    denominator = total_all * carried + jnp.sum(new_weights, axis=-1)
    new_part = jnp.einsum(
        "bgqs,bsgd->bgqd",
        new_weights.astype(jnp.bfloat16),
        fresh_values,
        preferred_element_type=jnp.float32,
    )
    numerator = sum_all * carried[..., None] + new_part
    attended = to_columns(numerator / denominator[..., None], step_number, group_count).astype(
        jnp.bfloat16
    )
    attended_part = lax.dynamic_slice_in_dim(attended, column_begin, feature_rows, 1)
    first_expert = lax.axis_index("tp") * gate_up_weight.shape[0]
    chosen = expert_ids.reshape(token_rows, -1)
    shares = combine_weights.reshape(token_rows, -1).astype(jnp.float32) / 65536.0
    head_terms = jnp.dot(attended_part, out_weight, preferred_element_type=jnp.float32)
    projected_rows = lax.psum(head_terms, "tp")
    residual = inputs_flat.astype(jnp.float32) + projected_rows
    normed_second = rms_rows(residual).astype(jnp.bfloat16)
    mixture = lax.psum(
        expert_terms(
            normed_second, chosen, shares, gate_up_weight, down_weight, first_expert
        ).astype(jnp.bfloat16),
        "tp",
    ).astype(jnp.float32)
    final_result = (residual + mixture).astype(jnp.bfloat16)
    return final_result.reshape(request_list, step_number, model_width)


def solution(mesh):
    in_specs = (
        P("req", None, None),
        P("req"),
        P("tp", None),
        P("req", "tp", None),
        P("req", "tp", None),
        P("tp", None),
        P("req", None, None),
        P("req", None, None),
        P("tp", None, None),
        P("tp", None, None),
    )
    out_specs = P("req", None, None)
    return jax.shard_map(
        per_device, mesh=mesh, in_specs=in_specs, out_specs=out_specs, check_vma=False
    )
```

profile of v0, /device:TPU:0, one launch (start us, length us, event | category | flops | bytes accessed | tf_op | source)
XLA Modules:
  0.0 358.4 jit_solution(16797033778908578031)
XLA Ops:
  10.0 1.1 fusion.13
  11.1 26.0 %all-gather.3 = bf16[32,64,16]{1,2,0:T(8,128)(2,1)S(1)} all-gather(bf16[1,64,16]{1,2,0:T(8,128)(2,1)S(1)} %fusion.13), channel_id=1, replica_groups=mesh['req'=4,'tp'=32] {'tp'}, dimensions={0}, use_global_device_ids=true | all-gather | bytes 67584 | tf_op jit(solution)/shard_map/all_gather | solution.py:103
  38.2 1.3 copy.24
  39.8 1.1 fusion.17
  42.7 24.2 %all-gather.1 = f32[128,8,8]{2,1,0:T(8,128)S(1)} all-gather(f32[4,8,8]{2,1,0:T(8,128)S(1)} %fusion.16), channel_id=3, replica_groups=mesh['req'=4,'tp'=32] {'tp'}, dimensions={0}, use_global_device_ids=true | all-gather | bytes 33792 | tf_op jit(solution)/shard_map/all_gather | solution.py:15
  67.0 22.6 %all-gather = f32[128,8,8]{2,1,0:T(8,128)S(1)} all-gather(f32[4,8,8]{2,1,0:T(8,128)S(1)} %get-tuple-element.216), channel_id=2, replica_groups=mesh['req'=4,'tp'=32] {'tp'}, dimensions={0}, use_global_device_ids=true | all-gather | bytes 33792 | tf_op jit(solution)/shard_map/all_gather | solution.py:15
  91.5 34.9 %while.19 = (s32[]{:T(128)}, f32[4,8,8]{2,1,0:T(8,128)S(1)}, f32[4,8,8]{2,1,0:T(8,128)S(1)}, f32[4,8,8,64]{3,2,1,0:T(8,128)S(1)}, f32[32,4,8,8]{3,2,1,0:T(8,128)...) while((s32[]{:T(128)}, f32[4,8,8]{2,1,0:T(8,128)S(1)}, ...), condition=%wide.region_4.5_spmd, body=%wide.region_3.4_spmd.sunk | while | flops 50693 | bytes 206991 | solution.py:20
  91.6 1.1 fusion.57
  92.7 1.1 fusion.57
  93.8 1.1 fusion.57
  95.0 1.1 fusion.57
  96.1 1.1 fusion.57
  97.2 1.1 fusion.57
  99.5 1.1 fusion.57
  100.6 1.1 fusion.57
  101.7 1.1 fusion.57
  102.9 1.1 fusion.57
  104.0 1.1 fusion.57
  105.1 1.1 fusion.57
  106.2 1.1 fusion.57
  107.4 1.1 fusion.57
  109.6 1.1 fusion.57
  130.0 93.8 %all-reduce.2.cloned.1.call-done = f32[16,1024]{1,0:T(8,128)} async-done(((f32[16,1024]{1,0:T(8,128)}), f32[16,1024]{1,0:T(8,128)}) %all-reduce.2.cloned.1.call-update) | async-done | bytes 65552 | tf_op jit(solution)/shard_map/psum | solution.py:186
  225.5 125.4 %psum.15 = bf16[16,1024]{1,0:T(8,128)(2,1)S(1)} all-reduce(bf16[16,1024]{1,0:T(8,128)(2,1)S(1)} %fusion.12), channel_id=1, replica_groups=mesh['req'=4,'tp'=32] {'tp'}, use_global_device_ids=true, to_apply=%region_10.11 | all-reduce | flops 16384 | bytes 65536 | tf_op jit(solution)/shard_map/psum | solution.py:189
  (109 shorter events, 32.2 us)
Async XLA Ops:
  6.5 218.2 %copy-start = (bf16[1,1024,1024]{2,1,0:T(8,128)(2,1)S(1)}, bf16[1,1024,1024]{2,1,0:T(8,128)(2,1)}, u32[]{:S(2)}) copy-start(bf16[1,1024,1024]{2,1,0:T(8,128)(2,1)} %param.20) | copy-start | bytes 6291460
  6.5 31.4 %copy-start.2 = (bf16[4,128,512]{2,1,0:T(8,128)(2,1)S(1)}, bf16[4,128,512]{2,1,0:T(8,128)(2,1)}, u32[]{:S(2)}) copy-start(bf16[4,128,512]{2,1,0:T(8,128)(2,1)} %param.15) | copy-start | bytes 1572868
  6.5 84.1 %all-gather.6.cloned.1.call-start = ((), (), s32[]{:S(2)}) async-start(), calls=%async_computation.1 | async-start | bytes 4325376 | tf_op jit(solution)/shard_map/all_gather | solution.py:15
  40.9 182.9 %all-reduce.2.cloned.1.call-start = ((), (), s32[]{:S(2)}) async-start(), calls=%async_computation | async-start | bytes 131072 | tf_op jit(solution)/shard_map/psum | solution.py:186
  89.5 1.0 copy-start.4
  91.5 36.8 %copy-start.3 = (bf16[32,1024]{1,0:T(8,128)(2,1)S(1)}, bf16[32,1024]{1,0:T(8,128)(2,1)}, u32[]{:S(2)}) copy-start(bf16[32,1024]{1,0:T(8,128)(2,1)} %param.17) | copy-start | bytes 196612
  126.5 98.7 %copy-start.1 = (bf16[1,512,1024]{2,1,0:T(8,128)(2,1)S(1)}, bf16[1,512,1024]{2,1,0:T(8,128)(2,1)}, u32[]{:S(2)}) copy-start(bf16[1,512,1024]{2,1,0:T(8,128)(2,1)} %param.21) | copy-start | bytes 3145732
Sparse Core Ops, SparseCore 0:
  41.1 45.7 all-gather.5
  129.3 94.4 all-reduce.1
where the time goes:
time: 359 us; the launch traced here: 358 us
  blocking collectives  198 us (55%)
  waiting for transfers between devices  93.8 us (26%)
  other arithmetic  39.8 us (11%)
  between operations  13.6 us (4%)
  local copies, waits for them, and re-layouts  6.09 us (2%)
  matrix products  5.89 us (2%)
    psum x1, blocking collectives, per_device(): lax.psum(expert_terms(normed_second, chosen, shares, gate_up_weight, down...  125 us
    psum x1, waiting for transfers between devices, per_device(): projected_rows = lax.psum(head_terms, 'tp')  93.8 us
    all_gather x2, blocking collectives, merged(): gathered = jax.tree.map(lambda a: lax.all_gather(a, axis), part)  46.8 us
    add x31, other arithmetic, join_parts(): earlier[2] * scale_earlier[..., None] + later[2] * scale_later[..., None]  33.3 us
    all_gather x1, blocking collectives, per_device(): projected_all = lax.all_gather(projected_part, 'tp', axis=0, tiled=True)  26 us
  transfers between devices with their start and end apart: 2, of which 1 were waited for; matrix products, arithmetic and copies ran while one was open for 1% of the time, Pallas kernels for 0%

commit v1 on v0

--- a/solution.py
+++ b/solution.py
@@ -183,7 +183,7 @@
     chosen = expert_ids.reshape(token_rows, -1)
     shares = combine_weights.reshape(token_rows, -1).astype(jnp.float32) / 65536.0
     head_terms = jnp.dot(attended_part, out_weight, preferred_element_type=jnp.float32)
-    projected_rows = lax.psum(head_terms, "tp")
+    projected_rows = jnp.sum(lax.all_gather(head_terms, axis_name="tp"), axis=0)
     residual = inputs_flat.astype(jnp.float32) + projected_rows
     normed_second = rms_rows(residual).astype(jnp.bfloat16)
     mixture = lax.psum(

time: 359 us -> 311 us (0.87)
  waiting for transfers between devices: 93.8 us -> 42.4 us
    psum x1 -> x0, waiting for transfers between devices: 93.8 us -> none  [per_device(): projected_rows = lax.psum(head_terms, 'tp')]
    all_gather x0 -> x1, waiting for transfers between devices: none -> 42.3 us  [per_device(): projected_rows = jnp.sum(lax.all_gather(head_terms, axis_name='tp'), axis=0)]
  transfers between devices with their start and end apart: 2 -> 2, of which waited for: 1 -> 1; matrix products, arithmetic and copies ran while one was open for 1% -> 2% of each run, Pallas kernels for 0% -> 0%
where the time goes in v1:
time: 311 us; the launch traced here: 310 us
  blocking collectives  199 us (64%)
  waiting for transfers between devices  42.4 us (14%)
  other arithmetic  41.4 us (13%)
  between operations  13.6 us (4%)
  matrix products  6.52 us (2%)
  local copies, waits for them, and re-layouts  6.15 us (2%)
    psum x1, blocking collectives, per_device(): lax.psum(expert_terms(normed_second, chosen, shares, gate_up_weight, down...  126 us
    all_gather x2, blocking collectives, merged(): gathered = jax.tree.map(lambda a: lax.all_gather(a, axis), part)  47 us
    all_gather x1, waiting for transfers between devices, per_device(): projected_rows = jnp.sum(lax.all_gather(head_terms, axis_name='tp'), axis=0)  42.3 us
    add x31, other arithmetic, join_parts(): earlier[2] * scale_earlier[..., None] + later[2] * scale_later[..., None]  33.3 us
    all_gather x1, blocking collectives, per_device(): projected_all = lax.all_gather(projected_part, 'tp', axis=0, tiled=True)  26 us
  transfers between devices with their start and end apart: 2, of which 1 were waited for; matrix products, arithmetic and copies ran while one was open for 2% of the time, Pallas kernels for 0%

profile of v1, /device:TPU:0, one launch (start us, length us, event | category | flops | bytes accessed | tf_op | source)
XLA Modules:
  0.0 310.3 jit_solution(518869353712301778)
XLA Ops:
  10.0 1.1 fusion.13
  11.1 26.0 %all-gather.4 = bf16[32,64,16]{1,2,0:T(8,128)(2,1)S(1)} all-gather(bf16[1,64,16]{1,2,0:T(8,128)(2,1)S(1)} %fusion.13), channel_id=1, replica_groups=mesh['req'=4,'tp'=32] {'tp'}, dimensions={0}, use_global_device_ids=true | all-gather | bytes 67584 | tf_op jit(solution)/shard_map/all_gather | solution.py:103
  38.2 1.3 copy.24
  39.8 1.1 fusion.17
  43.3 24.2 %all-gather.1 = f32[128,8,8]{2,1,0:T(8,128)S(1)} all-gather(f32[4,8,8]{2,1,0:T(8,128)S(1)} %fusion.16), channel_id=3, replica_groups=mesh['req'=4,'tp'=32] {'tp'}, dimensions={0}, use_global_device_ids=true | all-gather | bytes 33792 | tf_op jit(solution)/shard_map/all_gather | solution.py:15
  67.5 22.8 %all-gather = f32[128,8,8]{2,1,0:T(8,128)S(1)} all-gather(f32[4,8,8]{2,1,0:T(8,128)S(1)} %get-tuple-element.214), channel_id=2, replica_groups=mesh['req'=4,'tp'=32] {'tp'}, dimensions={0}, use_global_device_ids=true | all-gather | bytes 33792 | tf_op jit(solution)/shard_map/all_gather | solution.py:15
  90.3 1.6 fusion.46
  92.9 34.9 %while.19 = (s32[]{:T(128)}, f32[4,8,8]{2,1,0:T(8,128)S(1)}, f32[4,8,8]{2,1,0:T(8,128)S(1)}, f32[4,8,8,64]{3,2,1,0:T(8,128)S(1)}, f32[32,4,8,8]{3,2,1,0:T(8,128)...) while((s32[]{:T(128)}, f32[4,8,8]{2,1,0:T(8,128)S(1)}, ...), condition=%wide.region_4.5_spmd, body=%wide.region_3.4_spmd.sunk | while | flops 50693 | bytes 206991 | solution.py:20
  93.0 1.1 fusion.57
  94.1 1.1 fusion.57
  95.2 1.1 fusion.57
  96.3 1.1 fusion.57
  97.5 1.1 fusion.57
  98.6 1.1 fusion.57
  99.7 1.1 fusion.57
  100.8 1.1 fusion.57
  102.0 1.1 fusion.57
  104.2 1.1 fusion.57
  105.3 1.1 fusion.57
  106.5 1.1 fusion.57
  107.6 1.1 fusion.57
  131.5 42.3 %all-gather.10.cloned.1.call-done = f32[512,1024]{1,0:T(8,128)} async-done(((f32[16,1024]{1,0:T(8,128)}), f32[512,1024]{1,0:T(8,128)}) %all-gather.10.cloned.1.call-update) | async-done | bytes 2097168 | tf_op jit(solution)/shard_map/all_gather | solution.py:186
  173.8 1.8 reduce_sum.63
  176.5 126.3 %psum.7 = bf16[16,1024]{1,0:T(8,128)(2,1)S(1)} all-reduce(bf16[16,1024]{1,0:T(8,128)(2,1)S(1)} %fusion.12), channel_id=1, replica_groups=mesh['req'=4,'tp'=32] {'tp'}, use_global_device_ids=true, to_apply=%region_10.11 | all-reduce | flops 16384 | bytes 65536 | tf_op jit(solution)/shard_map/psum | solution.py:189
  (119 shorter events, 33.2 us)
Async XLA Ops:
  6.5 169.3 %copy-start = (bf16[1,1024,1024]{2,1,0:T(8,128)(2,1)S(1)}, bf16[1,1024,1024]{2,1,0:T(8,128)(2,1)}, u32[]{:S(2)}) copy-start(bf16[1,1024,1024]{2,1,0:T(8,128)(2,1)} %param.20) | copy-start | bytes 6291460
  6.5 31.4 %copy-start.3 = (bf16[4,128,512]{2,1,0:T(8,128)(2,1)S(1)}, bf16[4,128,512]{2,1,0:T(8,128)(2,1)}, u32[]{:S(2)}) copy-start(bf16[4,128,512]{2,1,0:T(8,128)(2,1)} %param.15) | copy-start | bytes 1572868
  6.5 85.4 %all-gather.8.cloned.1.call-start = ((), (), s32[]{:S(2)}) async-start(), calls=%async_computation | async-start | bytes 4325376 | tf_op jit(solution)/shard_map/all_gather | solution.py:15
  9.8 30.0 %copy-start.6 = (pred[4,128]{1,0:T(4,128)(4,1)}, pred[4,128]{1,0:T(4,128)(4,1)S(1)}, u32[]{:S(2)}) copy-start(pred[4,128]{1,0:T(4,128)(4,1)S(1)} %broadcast_compare_fusion) | copy-start | bytes 1540
  40.9 132.9 %all-gather.10.cloned.1.call-start = ((), (), s32[]{:S(2)}) async-start(), calls=%async_computation.1 | async-start | bytes 2162688 | tf_op jit(solution)/shard_map/all_gather | solution.py:186
  90.3 2.6 copy-start.7
  92.0 35.9 %copy-start.5 = (f32[4,8,8]{2,1,0:T(8,128)S(1)}, f32[4,8,8]{2,1,0:T(8,128)}, u32[]{:S(2)}) copy-start(f32[4,8,8]{2,1,0:T(8,128)} %get-tuple-element.216) | copy-start | bytes 3076
  92.9 36.8 %copy-start.4 = (bf16[32,1024]{1,0:T(8,128)(2,1)S(1)}, bf16[32,1024]{1,0:T(8,128)(2,1)}, u32[]{:S(2)}) copy-start(bf16[32,1024]{1,0:T(8,128)(2,1)} %param.17) | copy-start | bytes 196612
  127.8 47.8 %copy-start.2 = (bf16[4,4,1024]{2,1,0:T(4,128)(2,1)S(1)}, bf16[4,4,1024]{2,1,0:T(4,128)(2,1)}, u32[]{:S(2)}) copy-start(bf16[4,4,1024]{2,1,0:T(4,128)(2,1)} %param.12) | copy-start | bytes 98308
  173.8 2.5 copy-start.1
Sparse Core Ops, SparseCore 0:
  41.1 45.7 all-gather.7
  130.7 43.0 all-gather.9
